TPU v7x, 32 devices: a whole 2x2x4 slice. The times are simulated.
32 devices in a mesh: group: 4 (over y, x), hash: 8 (over z, core).
Axes of the slice: x: 2, y: 2, z: 4, core: 2. Of those that a mesh axis runs over, the one named last changes fastest.
Arguments:
- pooled: bfloat16 [8, 512, 32, 256], P('hash', 'group'), may hold values from -0.375 to 0.375
- weight: bfloat16 [1024, 2048], replicated, may hold values from -0.1875 to 0.1875
- cotangent: bfloat16 [8, 512, 2048], P('hash', 'group'), may hold values from -6 to 6
- owners: int32 [8, 32, 512, 2], P('hash', 'group'), may hold values from 0 to 7, all different within a row; in each aligned block of 4096 rows (0 to 4095, 4096 to 8191, ..., all dimensions but the last counted through in order) at most 1365 rows name the same one
- local_rows: int32 [8, 32, 512, 2], P('hash', 'group'), may hold values from 0 to 511
- table: float32 [32, 4096, 256], P('group', 'hash'), may hold values from -0.625 to 0.625
- accum: float32 [32, 4096], P('group', 'hash'), may hold values from 0.05 to 2
Outputs:
- wgrad: bfloat16 [1024, 2048], replicated
- table_out: float32 [32, 4096, 256], P('group', 'hash')
- accum_out: float32 [32, 4096], P('group', 'hash')
Inputs may be any that keep to these rules, and one draw needn't show every extreme that they name: Among the rows of one device (aligned blocks of 4096 bags), no owner is named more than 1365 times, a bound that some block reaches; the 2 owners of one bag differ.
All inputs are finite; a program needn't handle non-finite values.
Results may differ from a plain program's by a relative error of at most 0.0059.
Values may be sent and summed in bfloat16 or wider, within the bound.
No kernel may reach another device: no remote copies, remote signals or barrier semaphores. Data moves between devices by JAX's collectives and lax.ppermute only.
A program may use at most 128 MiB of HBM per device.

v0:
```python
import math
import jax
import jax.numpy as jnp
from jax import lax
from jax.sharding import PartitionSpec as P


def local(pooled, weight, cotangent, owners, local_rows, table, accum):
    vectors = pooled[0]
    samples, feats, width = vectors.shape
    inter = jnp.einsum("sfe,sge->sfg", vectors, vectors, preferred_element_type=jnp.float32).astype(
        jnp.bfloat16
    )
    inter_rows = inter.reshape(samples, feats * feats)
    preact = jnp.dot(inter_rows, weight, preferred_element_type=jnp.float32)
    sigmoid_v = jax.nn.sigmoid(preact)
    dpre = (
        cotangent[0].astype(jnp.float32) * (sigmoid_v * (1.0 + preact * (1.0 - sigmoid_v)))
    ).astype(jnp.bfloat16)
    dinter = lax.dot_general(
        dpre, weight, (((1,), (1,)), ((), ())), preferred_element_type=jnp.float32
    ).reshape(samples, feats, feats)
    dsym = (dinter + jnp.swapaxes(dinter, 1, 2)).astype(jnp.bfloat16)
    dpooled = jnp.einsum("sfg,sge->fse", dsym, vectors, preferred_element_type=jnp.float32).astype(
        jnp.bfloat16
    )
    exchanged = lax.all_to_all(dpooled, "group", split_axis=0, concat_axis=1, tiled=True)
    wlocal = lax.dot_general(
        inter_rows, dpre, (((0,), (0,)), ((), ())), preferred_element_type=jnp.float32
    )
    total_samples = samples * lax.axis_size("group") * lax.axis_size("hash")
    wgrad = (lax.psum(wlocal, ("group", "hash")) / math.sqrt(total_samples)).astype(jnp.bfloat16)
    owner_ids = owners[0]
    row_ids = local_rows[0]
    groups_local, rows_dev = accum.shape
    hashes = lax.axis_size("hash")
    feature_index = jnp.arange(groups_local, dtype=jnp.int32)[:, None, None]
    values = jnp.broadcast_to(exchanged[:, :, None, :], owner_ids.shape + (width,)).reshape(
        -1, width
    )
    dense_keys = (feature_index * (hashes * rows_dev) + owner_ids * rows_dev + row_ids).reshape(-1)
    partial_grad = jax.ops.segment_sum(
        values.astype(jnp.float32), dense_keys, num_segments=groups_local * hashes * rows_dev
    )
    rowgrad = lax.psum_scatter(
        partial_grad.reshape(groups_local, hashes * rows_dev, width).astype(jnp.bfloat16),
        "hash",
        scatter_dimension=1,
        tiled=True,
    ).astype(jnp.float32)
    accum_out = accum + jnp.mean(rowgrad * rowgrad, axis=-1)
    table_out = table - 0.1 * rowgrad / jnp.sqrt(accum_out)[:, :, None]
    return (wgrad, table_out, accum_out)


def solution(mesh):
    in_specs = (
        P("hash", "group", None, None),
        P(),
        P("hash", "group", None),
        P("hash", "group", None, None),
        P("hash", "group", None, None),
        P("group", "hash", None),
        P("group", "hash"),
    )
    out_specs = (P(), P("group", "hash", None), P("group", "hash"))
    return jax.shard_map(local, mesh=mesh, in_specs=in_specs, out_specs=out_specs, check_vma=False)
```

profile of v0, /device:TPU:0, one launch (start us, length us, event | category | flops | bytes accessed | tf_op | source)
XLA Modules:
  0.0 382.3 jit_solution(6259762305518760065)
XLA Ops:
  8.0 0.0 all-reduce.2.cloned.1.call-start
  8.1 1.5 copy-done
  9.6 0.7 fusion.11
  10.3 1.1 copy.25
  11.4 3.0 fusion.27
  14.4 4.6 %fusion.17 = f32[1024,2048]{1,0:T(8,128)} fusion(bf16[128,1024]{0,1:T(8,128)(2,1)S(1)} %bitcast.47, f32[128,2048]{1,0:T(8,128)S(1)} %fusion.27, bf16[1,128,2048]{2,1,0:T(8,128)(2,1)S(1)} %copy-done.2), kind=kOutput, calls=%fused_computation.19 | convolution fusion | flops 539492352 | bytes 10223616 | tf_op jit(solution)/shard_map/dot_general | solution.py:28
  19.0 3.7 fusion.15
  22.7 0.3 fusion.21
  23.0 1.4 copy.30
  24.5 0.7 convert_bitcast_fusion.1
  25.2 2.6 copy.31
  27.7 5.1 %all-to-all-start = ((bf16[32,128,256]{2,1,0:T(8,128)(2,1)}), bf16[32,128,256]{2,1,0:T(8,128)(2,1)S(1)}, u32[]{:S(2)}, u32[]{:S(2)}) async-start(bf16[32,128,256]{2,1,0:T(8,128)(2,1)} %copy.31), calls=%async_computation | async-start | bytes 4194304 | tf_op jit(solution)/shard_map/all_to_all | solution.py:27
  32.9 2.0 copy.26
  34.9 3.1 mul.48
  38.0 1.5 add.47
  39.6 3.0 add.48
  42.6 2.0 copy.27
  44.6 3.0 squeeze.9
  47.7 20.9 %all-to-all-done = bf16[32,128,256]{2,1,0:T(8,128)(2,1)S(1)} async-done(((bf16[32,128,256]{2,1,0:T(8,128)(2,1)}), bf16[32,128,256]{2,1,0:T(8,128)(2,1)S(1)}, u32[]{:S(2)}, u32[]{:S(2)}) %all-to-all-start) | async-done | bytes 2097184 | tf_op jit(solution)/shard_map/all_to_all | solution.py:27
  68.6 0.5 convert_bitcast_fusion
  69.1 0.4 copy.32
  69.6 4.5 %broadcast_in_dim.5 = f32[8,512,2,256]{3,2,1,0:T(2,128)} broadcast(f32[8,512,256]{2,1,0:T(8,128)S(1)} %bitcast.44), dimensions={0,1,3} | broadcast | bytes 12582912 | tf_op jit(solution)/shard_map/broadcast_in_dim | solution.py:38
  74.0 11.1 %reshape.73 = f32[8192,256]{1,0:T(8,128)} reshape(f32[8,512,2,256]{3,2,1,0:T(2,128)} %broadcast_in_dim.5) | data formatting | bytes 16777216 | tf_op jit(solution)/shard_map/convert_element_type | solution.py:43
  85.2 58.1 %scatter_custom_fusion = f32[32768,256]{1,0:T(8,128)} fusion(s32[8192]{0:T(1024)S(1)} %bitcast.49, f32[8192,256]{1,0:T(8,128)} %reshape.73, f32[]{:T(128)} %constant.3.clone.1), kind=kCustom, calls=%fused_computation.1 | custom fusion | flops 2097152 | bytes 33554944 | tf_op jit(solution)/shard_map/scatter-add | solution.py:42
  143.3 17.5 %convert_element_type.62 = bf16[32768,256]{1,0:T(8,128)(2,1)} convert(f32[32768,256]{1,0:T(8,128)} %scatter_custom_fusion) | non-fusion elementwise | flops 8388608 | bytes 50331648 | tf_op jit(solution)/shard_map/convert_element_type | solution.py:46
  160.7 0.0 reduce-scatter.2.cloned.1.call-update
  160.8 115.0 %all-reduce.2.cloned.1.call-done = f32[1024,2048]{1,0:T(8,128)} async-done(((f32[1024,2048]{1,0:T(8,128)}), f32[1024,2048]{1,0:T(8,128)}) %all-reduce.2.cloned.1.call-update) | async-done | bytes 8388624 | tf_op jit(solution)/shard_map/psum | solution.py:32
  275.7 6.6 %multiply_convert_fusion = bf16[1024,2048]{1,0:T(8,128)(2,1)} fusion(f32[1024,2048]{1,0:T(8,128)} %all-reduce.2.cloned.1.call-done), kind=kLoop, calls=%fused_computation.3 | loop fusion | flops 4194304 | bytes 12582912 | tf_op jit(solution)/shard_map/convert_element_type | solution.py:32
  282.3 85.0 %reduce-scatter.2.cloned.1.call-done = bf16[8,512,256]{2,1,0:T(8,128)(2,1)} async-done(((bf16[8,4096,256]{2,1,0:T(8,128)(2,1)}), bf16[8,512,256]{2,1,0:T(8,128)(2,1)}) %reduce-scatter.2.cloned.1.call-update) | async-done | bytes 2097168 | tf_op jit(solution)/shard_map/reduce_scatter | solution.py:45
  367.4 2.2 fusion.4
  369.6 0.6 fusion.26
  370.2 4.6 %fusion.3 = f32[8,512,256]{2,1,0:T(8,128)} fusion(f32[8,512,256]{2,1,0:T(8,128)} %param.12, bf16[8,512,256]{2,1,0:T(8,128)(2,1)} %reduce-scatter.2.cloned.1.call-done, f32[8,512]{1,0:T(8,128)S(1)} %get-tuple-element.3), kind=kLoop, calls=%fused_computation.7 | loop fusion | flops 4194304 | bytes 10502144 | tf_op jit(solution)/shard_map/sub | solution.py:52
  (16 shorter events, 0.1 us)
Async XLA Ops:
  8.0 1.6 copy-start
  8.0 267.7 %all-reduce.2.cloned.1.call-start = ((), (), s32[]{:S(2)}) async-start(), calls=%async_computation.2 | async-start | bytes 16777216 | tf_op jit(solution)/shard_map/psum | solution.py:32
  11.4 3.0 copy-start.2
  25.1 7.7 %copy-start.4 = (s32[1,8,512,2]{2,3,1,0:T(2,128)S(1)}, s32[1,8,512,2]{2,3,1,0:T(2,128)}, u32[]{:S(2)}) copy-start(s32[1,8,512,2]{2,3,1,0:T(2,128)} %param.10) | copy-start | bytes 98308
  27.7 40.9 %all-to-all-start = ((bf16[32,128,256]{2,1,0:T(8,128)(2,1)}), bf16[32,128,256]{2,1,0:T(8,128)(2,1)S(1)}, u32[]{:S(2)}, u32[]{:S(2)}) async-start(bf16[32,128,256]{2,1,0:T(8,128)(2,1)} %copy.31), calls=%async_computation | async-start | bytes 4194304 | tf_op jit(solution)/shard_map/all_to_all | solution.py:27
  32.9 334.5 %reduce-scatter.2.cloned.1.call-start = ((), (), s32[]{:S(2)}) async-start(), calls=%async_computation.3 | async-start | bytes 18874368 | tf_op jit(solution)/shard_map/reduce_scatter | solution.py:45
  32.9 9.7 %copy-start.3 = (s32[1,8,512,2]{2,3,1,0:T(2,128)S(1)}, s32[1,8,512,2]{2,3,1,0:T(2,128)}, u32[]{:S(2)}) copy-start(s32[1,8,512,2]{2,3,1,0:T(2,128)} %param.11) | copy-start | bytes 98308
  160.8 208.8 %copy-start.5 = (f32[8,512]{1,0:T(8,128)S(1)}, f32[8,512]{1,0:T(8,128)}, u32[]{:S(2)}) copy-start(f32[8,512]{1,0:T(8,128)} %param.13) | copy-start | bytes 49156
  370.2 4.6 %copy-start.1 = (bf16[1,128,32,256]{3,2,1,0:T(8,128)(2,1)S(1)}, bf16[1,128,32,256]{3,2,1,0:T(8,128)(2,1)}, u32[]{:S(2)}) copy-start(bf16[1,128,32,256]{3,2,1,0:T(8,128)(2,1)} %param.7) | copy-start | bytes 6291460
Sparse Core Ops, SparseCore 0:
  19.1 256.6 all-reduce.1
Sparse Core Ops, SparseCore 1:
  160.8 206.5 reduce-scatter.1
where the time goes:
time: 383 us; the launch traced here: 382 us
  waiting for transfers between devices  221 us (58%)
  other arithmetic  90.5 us (24%)
  local copies, waits for them, and re-layouts  37.4 us (10%)
  between operations  15.6 us (4%)
  matrix products  12.6 us (3%)
  starting transfers between devices  5.15 us (1%)
    psum x1, waiting for transfers between devices, local(): lax.psum(wlocal, ('group', 'hash')) / math.sqrt(total_samples)  115 us
    reduce_scatter x1, waiting for transfers between devices, local(): lax.psum_scatter(partial_grad.reshape(groups_local, hashes * rows_dev, wi...  85 us
    scatter-add x1, other arithmetic, local(): jax.ops.segment_sum(values.astype(jnp.float32), dense_keys, num_segments=...  58.1 us
    all_to_all x1, waiting for transfers between devices, local(): lax.all_to_all(dpooled, 'group', split_axis=0, concat_axis=1, tiled=True)  20.9 us
    convert_element_type x1, other arithmetic, local(): partial_grad.reshape(groups_local, hashes * rows_dev, width)  17.5 us
    convert_element_type x2, local copies, waits for them, and re-layouts, local(): values.astype(jnp.float32)  11.6 us
  transfers between devices with their start and end apart: 3, of which 3 were waited for; matrix products, arithmetic and copies ran while one was open for 32% of the time, Pallas kernels for 0%

commit v1 on v0

--- a/solution.py
+++ b/solution.py
@@ -29,7 +29,9 @@
         inter_rows, dpre, (((0,), (0,)), ((), ())), preferred_element_type=jnp.float32
     )
     total_samples = samples * lax.axis_size("group") * lax.axis_size("hash")
-    wgrad = (lax.psum(wlocal, ("group", "hash")) / math.sqrt(total_samples)).astype(jnp.bfloat16)
+    wgrad = (lax.psum(lax.psum(wlocal, "group"), "hash") / math.sqrt(total_samples)).astype(
+        jnp.bfloat16
+    )
     owner_ids = owners[0]
     row_ids = local_rows[0]
     groups_local, rows_dev = accum.shape

time: 383 us -> 557 us (1.45)
  waiting for transfers between devices: 221 us -> 398 us
    psum x1 -> x2, waiting for transfers between devices: 115 us -> 224 us  [the longest x1 175 us: local(): lax.psum(wlocal, 'group')]
    reduce_scatter x1, waiting for transfers between devices: 85 us -> 164 us  [local(): lax.psum_scatter(partial_grad.reshape(groups_local, hashes * rows_dev, wi...]
    all_to_all x1, waiting for transfers between devices: 20.9 us -> 9.92 us  [local(): lax.all_to_all(dpooled, 'group', split_axis=0, concat_axis=1, tiled=True)]
  transfers between devices with their start and end apart: 3 -> 4, of which waited for: 3 -> 4; matrix products, arithmetic and copies ran while one was open for 32% -> 22% of each run, Pallas kernels for 0% -> 0%
where the time goes in v1:
time: 557 us; the launch traced here: 556 us
  waiting for transfers between devices  398 us (71%)
  other arithmetic  90.3 us (16%)
  local copies, waits for them, and re-layouts  37.2 us (7%)
  between operations  13.9 us (2%)
  matrix products  12.6 us (2%)
    psum x1, waiting for transfers between devices, local(): lax.psum(wlocal, 'group')  175 us
    reduce_scatter x1, waiting for transfers between devices, local(): lax.psum_scatter(partial_grad.reshape(groups_local, hashes * rows_dev, wi...  164 us
    scatter-add x1, other arithmetic, local(): jax.ops.segment_sum(values.astype(jnp.float32), dense_keys, num_segments=...  58.1 us
    psum x1, waiting for transfers between devices, local(): lax.psum(lax.psum(wlocal, 'group'), 'hash') / math.sqrt(total_samples)  49.4 us
    convert_element_type x1, other arithmetic, local(): partial_grad.reshape(groups_local, hashes * rows_dev, width)  17.3 us
    convert_element_type x2, local copies, waits for them, and re-layouts, local(): values.astype(jnp.float32)  11.5 us
  transfers between devices with their start and end apart: 4, of which 4 were waited for; matrix products, arithmetic and copies ran while one was open for 22% of the time, Pallas kernels for 0%

profile of v1, /device:TPU:0, one launch (start us, length us, event | category | flops | bytes accessed | tf_op | source)
XLA Modules:
  0.0 556.4 jit_solution(6411775365708089196)
XLA Ops:
  7.2 1.5 copy-done
  8.8 0.7 fusion.11
  9.4 1.1 copy.25
  10.5 3.0 fusion.27
  13.5 4.6 fusion.17
  18.2 174.9 %all-reduce.3.cloned.1.call-done = f32[1024,2048]{1,0:T(8,128)} async-done(((f32[1024,2048]{1,0:T(8,128)}), f32[1024,2048]{1,0:T(8,128)}) %all-reduce.3.cloned.1.call-update) | async-done | bytes 8388624 | tf_op jit(solution)/shard_map/psum | solution.py:32
  193.1 3.7 fusion.15
  196.8 0.3 fusion.21
  197.1 1.4 copy.30
  198.6 0.7 convert_bitcast_fusion.1
  199.3 2.5 copy.31
  201.8 3.6 all-to-all-start
  205.4 0.2 reduce-scatter.2.cloned.1.call-start
  205.7 2.0 copy.26
  207.7 3.1 mul.48
  210.8 1.5 add.49
  212.3 3.0 add.50
  215.3 2.0 copy.27
  217.3 3.0 squeeze.9
  220.4 9.9 %all-to-all-done = bf16[32,128,256]{2,1,0:T(8,128)(2,1)S(1)} async-done(((bf16[32,128,256]{2,1,0:T(8,128)(2,1)}), bf16[32,128,256]{2,1,0:T(8,128)(2,1)S(1)}, u32[]{:S(2)}, u32[]{:S(2)}) %all-to-all-start) | async-done | bytes 2097184 | tf_op jit(solution)/shard_map/all_to_all | solution.py:27
  230.3 0.5 convert_bitcast_fusion
  230.9 0.4 copy.32
  231.3 4.5 broadcast_in_dim.5
  235.8 11.0 %reshape.73 = f32[8192,256]{1,0:T(8,128)} reshape(f32[8,512,2,256]{3,2,1,0:T(2,128)} %broadcast_in_dim.5) | data formatting | bytes 16777216 | tf_op jit(solution)/shard_map/convert_element_type | solution.py:45
  246.8 58.1 %scatter_custom_fusion = f32[32768,256]{1,0:T(8,128)} fusion(s32[8192]{0:T(1024)S(1)} %bitcast.49, f32[8192,256]{1,0:T(8,128)} %reshape.73, f32[]{:T(128)} %constant.3.clone.1), kind=kCustom, calls=%fused_computation.1 | custom fusion | flops 2097152 | bytes 33554944 | tf_op jit(solution)/shard_map/scatter-add | solution.py:44
  304.9 17.3 %convert_element_type.62 = bf16[32768,256]{1,0:T(8,128)(2,1)} convert(f32[32768,256]{1,0:T(8,128)} %scatter_custom_fusion) | non-fusion elementwise | flops 8388608 | bytes 50331648 | tf_op jit(solution)/shard_map/convert_element_type | solution.py:48
  322.3 49.4 %all-reduce.5.cloned.1.call-done = f32[1024,2048]{1,0:T(8,128)} async-done(((f32[1024,2048]{1,0:T(8,128)}), f32[1024,2048]{1,0:T(8,128)}) %all-reduce.5.cloned.1.call-update) | async-done | bytes 8388624 | tf_op jit(solution)/shard_map/psum | solution.py:32
  371.7 6.5 %multiply_convert_fusion = bf16[1024,2048]{1,0:T(8,128)(2,1)} fusion(f32[1024,2048]{1,0:T(8,128)} %all-reduce.5.cloned.1.call-done), kind=kLoop, calls=%fused_computation.3 | loop fusion | flops 4194304 | bytes 12582912 | tf_op jit(solution)/shard_map/convert_element_type | solution.py:32
  378.2 164.1 %reduce-scatter.2.cloned.1.call-done = bf16[8,512,256]{2,1,0:T(8,128)(2,1)} async-done(((bf16[8,4096,256]{2,1,0:T(8,128)(2,1)}), bf16[8,512,256]{2,1,0:T(8,128)(2,1)}) %reduce-scatter.2.cloned.1.call-update) | async-done | bytes 2097168 | tf_op jit(solution)/shard_map/reduce_scatter | solution.py:47
  542.4 2.2 fusion.4
  544.6 0.6 fusion.26
  545.2 4.6 fusion.3
  (19 shorter events, 0.2 us)
Async XLA Ops:
  7.2 1.6 copy-start
  7.2 185.9 %all-reduce.3.cloned.1.call-start = ((), (), s32[]{:S(2)}) async-start(), calls=%async_computation.2 | async-start | bytes 16777216 | tf_op jit(solution)/shard_map/psum | solution.py:32
  10.5 3.0 copy-start.2
  18.1 353.5 %all-reduce.5.cloned.1.call-start = ((), (), s32[]{:S(2)}) async-start(), calls=%async_computation.3 | async-start | bytes 16777216 | tf_op jit(solution)/shard_map/psum | solution.py:32
  199.3 6.4 %copy-start.4 = (s32[1,8,512,2]{2,3,1,0:T(2,128)S(1)}, s32[1,8,512,2]{2,3,1,0:T(2,128)}, u32[]{:S(2)}) copy-start(s32[1,8,512,2]{2,3,1,0:T(2,128)} %param.10) | copy-start | bytes 98308
  201.8 28.6 %all-to-all-start = ((bf16[32,128,256]{2,1,0:T(8,128)(2,1)}), bf16[32,128,256]{2,1,0:T(8,128)(2,1)S(1)}, u32[]{:S(2)}, u32[]{:S(2)}) async-start(bf16[32,128,256]{2,1,0:T(8,128)(2,1)} %copy.31), calls=%async_computation | async-start | bytes 4194304 | tf_op jit(solution)/shard_map/all_to_all | solution.py:27
  205.4 337.0 %reduce-scatter.2.cloned.1.call-start = ((), (), s32[]{:S(2)}) async-start(), calls=%async_computation.4 | async-start | bytes 18874368 | tf_op jit(solution)/shard_map/reduce_scatter | solution.py:47
  205.7 9.7 %copy-start.3 = (s32[1,8,512,2]{2,3,1,0:T(2,128)S(1)}, s32[1,8,512,2]{2,3,1,0:T(2,128)}, u32[]{:S(2)}) copy-start(s32[1,8,512,2]{2,3,1,0:T(2,128)} %param.11) | copy-start | bytes 98308
  322.3 222.3 %copy-start.5 = (f32[8,512]{1,0:T(8,128)S(1)}, f32[8,512]{1,0:T(8,128)}, u32[]{:S(2)}) copy-start(f32[8,512]{1,0:T(8,128)} %param.13) | copy-start | bytes 49156
  545.2 4.6 copy-start.1
Sparse Core Ops, SparseCore 0:
  18.3 174.7 all-reduce.2
  195.4 176.2 all-reduce.4
  374.0 168.2 reduce-scatter.1
